TPU v7x, 32 devices: a whole 2x2x4 slice. The times are simulated.
32 devices in a mesh: group: 4 (over z), sub: 8 (over y, x, core).
Axes of the slice: x: 2, y: 2, z: 4, core: 2. Of those that a mesh axis runs over, the one named last changes fastest.
Arguments:
- modal_dofs: float32 [9, 35, 4096], P(None, None, ('group', 'sub')), may hold values from -6 to 6
- jacobians: float32 [3, 9, 9, 4096], P(None, None, None, ('group', 'sub')), may hold values from -1.25 to 1.25
- stiffness: float32 [3, 35, 35], replicated, may hold values from -1 to 1
- face_trace: float32 [4, 15, 35], replicated, may hold values from -1 to 1
- neighbour_trace: float32 [12, 15, 35], replicated, may hold values from -1 to 1
- own_flux: float32 [4, 9, 9, 4096], P(None, None, None, ('group', 'sub')), may hold values from -2 to 2
- neighbour_flux: float32 [4, 9, 9, 4096], P(None, None, None, ('group', 'sub')), may hold values from -2 to 2
- face_lift: float32 [4, 35, 15], replicated, may hold values from -0.75 to 0.75
- neighbour_code: int32 [4, 4096], P(None, ('group', 'sub')), may hold values from 0 to 1663, as said below
- rim_select: int32 [4096], P(('group', 'sub')), may hold values from 0 to 1535
- fault_element: int32 [2, 1024], P(None, ('group', 'sub')), may hold values from 0 to 127
- fault_face: int32 [2, 1024], P(None, ('group', 'sub')), may hold values from 0 to 3
- send_count: int32 [4, 32], P(None, ('group', 'sub')), may hold values from 0 to 8
- fault_trace: float32 [4, 49, 35], replicated, may hold values from -1 to 1
- fault_lift: float32 [4, 35, 49], replicated, may hold values from -0.875 to 0.875
- coupling: float32 [9, 2], replicated, may hold values from -4 to 4
- fault_state: float32 [49, 1024], P(None, ('group', 'sub')), may hold values from -1 to 1
- direct_effect: float32 [49, 1024], P(None, ('group', 'sub')), may hold values from 0.5 to 1.5
- evolution_rate: float32 [49, 1024], P(None, ('group', 'sub')), may hold values from 0.5 to 2
Outputs:
- new_dofs: float32 [9, 35, 4096], P(None, None, ('group', 'sub'))
- new_state: float32 [49, 1024], P(None, ('group', 'sub'))
Inputs may be any that keep to these rules, and one draw needn't show every extreme that they name: `neighbour_code`: face 0 of local elements 0 to 127 reads neighbour-list row 1536 plus its local index; other entries are any row below 1536.
All inputs are finite; a program needn't handle non-finite values.
Results may differ from a plain program's by a relative error of at most 0.0003.
Values sent between devices are 32-bit elements; how exact they have to be, the bound alone decides.
A program may use at most 128 MiB of HBM per device.

v0:
```python
import functools

import jax
import jax.numpy as jnp
from jax import lax
from jax.experimental import pallas as pl
from jax.experimental.pallas import tpu as pltpu
from jax.sharding import PartitionSpec as P

DERIV = 4
NEWTON = 3
CAP = 8
F32 = jnp.float32
BF16 = jnp.bfloat16
MESH = pl.DeviceIdType.MESH


def up(n, m):
    return (n + m - 1) // m * m


def halves(x):
    high = x.astype(BF16).astype(F32)
    return high, x - high


def stacked(parts, rows):
    have = sum(p.shape[0] for p in parts)
    if have < rows:
        parts = parts + [jnp.zeros((rows - have, parts[0].shape[1]), F32)]
    return jnp.concatenate(parts, axis=0).astype(BF16)


def mul(a, b):
    return lax.dot_general(a, b, (((1,), (0,)), ((), ())), preferred_element_type=F32)


def roll(x, shift):
    return pltpu.roll(x, shift, 1)


def lanes3(a, step):
    high, low = halves(a)
    return (high + roll(low, step) + roll(high, 2 * step)).astype(BF16)


def kernel(
    n_group,
    n_sub,
    dofs,
    jac,
    stiff,
    face_trace,
    neighbour_trace,
    own_flux_hbm,
    neighbour_flux_hbm,
    face_lift,
    code,
    rim,
    fault_element,
    fault_face,
    send_count,
    fault_trace,
    fault_lift,
    coupling,
    fault_state,
    direct_effect,
    evolution_rate,
    out,
    out_state,
    integ,
    parts,
    table,
    own,
    near,
    flux,
    base,
    w_stiff,
    w_face,
    w_near,
    w_ftrace,
    w_flift,
    w_lift,
    w_state,
    rim_send,
    rim_recv,
    fric_send,
    fric_recv,
    slip_send,
    slip_recv,
    own_flux,
    neighbour_flux,
    stage_sem,
    send_sem,
    recv_sem,
):
    staged = [
        pltpu.make_async_copy(own_flux_hbm, own_flux, stage_sem.at[0]),
        pltpu.make_async_copy(neighbour_flux_hbm, neighbour_flux, stage_sem.at[1]),
    ]
    for copy in staged:
        copy.start()
    nf, nb, elems = dofs.shape
    ndim = stiff.shape[0]
    nfm, nj, _ = face_trace.shape
    nk = neighbour_trace.shape[0]
    _, nface, nq = fault_trace.shape
    slots = fault_element.shape[1]
    cp, fp, qp = up(nb, 8), up(nfm, 8), up(nq, 8)
    width = 4 * slots
    me_g = lax.axis_index("group")
    me_s = lax.axis_index("sub")
    prev_s = lax.rem(me_s + n_sub - 1, n_sub)
    next_s = lax.rem(me_s + 1, n_sub)

    barrier = pltpu.get_barrier_semaphore()
    for d in range(1, n_group):
        pl.semaphore_signal(
            barrier, inc=1, device_id=(lax.rem(me_g + d, n_group), me_s), device_id_type=MESH
        )
    for s in (prev_s, next_s):
        pl.semaphore_signal(barrier, inc=1, device_id=(me_g, s), device_id_type=MESH)

    w_stiff[...] = jnp.zeros_like(w_stiff)
    w_face[...] = jnp.zeros_like(w_face)
    w_near[...] = jnp.zeros_like(w_near)
    w_ftrace[...] = jnp.zeros_like(w_ftrace)
    w_flift[...] = jnp.zeros_like(w_flift)
    w_lift[...] = jnp.zeros_like(w_lift)
    for d in range(ndim):
        w_stiff[d * cp : d * cp + nb, :nb] = stiff[d]
    for k in range(nface):
        for b in range(nb):
            w_ftrace[k, b : b + 1, :nq] = fault_trace[b, pl.ds(k, 1), :]
            w_flift[k * cp + b : k * cp + b + 1, :nq] = fault_lift[b, pl.ds(k, 1), :]
    for k in range(nk):
        w_near[k * fp : k * fp + nfm, :nb] = neighbour_trace[k]
    for j in range(nj):
        for q in range(nfm):
            w_face[j * fp + q : j * fp + q + 1, :nb] = face_trace[q, pl.ds(j, 1), :]
            w_lift[j * fp + q : j * fp + q + 1, :nb] = face_lift[q, pl.ds(j, 1), :]
    w_state[0] = jnp.zeros(w_state.shape[1:], F32)
    w_state[1] = jnp.ones(w_state.shape[1:], F32)
    for i in range(4):
        w_state[0, i * slots : (i + 1) * slots, :nq] = fault_state[...]
        w_state[1, i * slots : (i + 1) * slots, :nq] = direct_effect[...]

    a_stiff = lanes3(-w_stiff[...], cp)

    gap = jnp.zeros((128 - cp, 128), F32)
    v = [jnp.concatenate([w_stiff[d * cp : (d + 1) * cp], gap], axis=0).T[:cp] for d in range(ndim)]
    a_last = jnp.concatenate(
        [lanes3(jnp.concatenate(v, axis=0), cp), lanes3(w_near[...], cp), lanes3(w_face[...], cp)],
        axis=0,
    )
    many = 3 if nf % 3 == 0 else 1
    rows = ndim * cp

    def spread_out(fields):
        out = []
        for x in fields:
            high, low = halves(x)
            out.append(stacked([high, high, low], 128))
        return jnp.concatenate(out, axis=1)

    def mixed(turn, f):
        sums = [None] * many
        for g in range(nf):
            for d in range(ndim):
                x = parts[turn, g, d * cp : (d + 1) * cp]
                for m in range(many):
                    term = jac[f + m, g, pl.ds(d, 1), :] * x
                    sums[m] = term if sums[m] is None else sums[m] + term
        return sums

    for f in range(0, nf, many):
        group = [
            jnp.concatenate([dofs[f + m], jnp.zeros((cp - nb, elems), F32)], axis=0)
            for m in range(many)
        ]
        r = mul(a_stiff, spread_out(group))
        for m in range(many):
            integ[f + m] = group[m]
            parts[0, f + m] = r[:, m * elems : (m + 1) * elems]

    factorial = 1.0
    for degree in range(1, DERIV + 1):
        factorial = factorial * (degree + 1)
        turn = (degree - 1) % 2
        for f in range(0, nf, many):
            group = mixed(turn, f)
            total = [integ[f + m] + group[m] / factorial for m in range(many)]
            for m in range(many):
                integ[f + m] = total[m]
            last = degree == DERIV
            r = mul(a_last if last else a_stiff, spread_out(total if last else group))
            for m in range(many):
                y = r[:, m * elems : (m + 1) * elems]
                parts[1 - turn, f + m] = y[:rows]
                if last:
                    table[f + m] = y[rows : rows + nk * fp]
                    y = y[rows + nk * fp :]
                    for j in range(nj):
                        own[j, f + m] = y[j * fp : (j + 1) * fp]

    lane = lax.broadcasted_iota(jnp.int32, (1, width), 1)
    is_v1 = (lane & slots) != 0
    sign_i = jnp.where((lane & (2 * slots)) != 0, 1.0, -1.0).astype(F32)
    slot_group = (lane & (slots - 1)) // CAP
    elem = fault_element[...]
    face = fault_face[...]
    elem_row = jnp.concatenate([elem[0:1], elem[0:1], elem[1:2], elem[1:2]], axis=1)
    face_row = jnp.concatenate([face[0:1], face[0:1], face[1:2], face[1:2]], axis=1)
    hit = lax.broadcasted_iota(jnp.int32, (elems, width), 0) == elem_row
    hot = jnp.where(hit, 1.0, 0.0).astype(F32)

    i0, i3, i7 = integ[0], integ[3], integ[7]
    highs, lows = zip(*[halves(x) for x in (i0, i3, i7)])
    g = mul(stacked(list(highs) + list(lows), 6 * cp), hot.astype(BF16))
    g = g[: 3 * cp] + g[3 * cp :]
    g0, g3, g7 = g[:cp], g[cp : 2 * cp], g[2 * cp :]
    a_fault = []
    for k in range(nface):
        high, low = halves(w_ftrace[k])
        gap = jnp.zeros((128 - 3 * cp, 128), F32)
        a_fault.append(jnp.concatenate([high, low, high, gap], axis=0).T[:qp])
    a_fault = jnp.concatenate(a_fault, axis=0).astype(BF16)

    def fault_sides(x):
        high, low = halves(x)
        y = mul(a_fault, stacked([high, high, low], 128))
        total = jnp.where(face_row == 0, y[:qp], 0.0)
        for k in range(1, nface):
            total = jnp.where(face_row == k, y[k * qp : (k + 1) * qp], total)
        return total

    mean = fault_sides(jnp.where(is_v1, 0.5 * g3 + (0.5 * sign_i) * g7, 0.5 * g0))
    mean = mean + roll(mean, 2 * slots)
    fric_send[...] = mean
    sides = fault_sides(jnp.where(is_v1, g7, g3))

    pl.semaphore_wait(barrier, n_group + 1)

    def exchange(src, dst, first):
        copies = []
        for d in range(1, n_group):
            copy = pltpu.make_async_remote_copy(
                src_ref=src,
                dst_ref=dst.at[d - 1],
                send_sem=send_sem.at[first + d - 1],
                recv_sem=recv_sem.at[first + d - 1],
                device_id=(lax.rem(me_g + d, n_group), me_s),
                device_id_type=MESH,
            )
            copy.start()
            copies.append(copy)
        return copies

    def gathered(mine, copies, dst):
        total = jnp.where(slot_group == me_g, mine, 0.0)
        for d, copy in enumerate(copies, 1):
            copy.wait_recv()
            other = lax.rem(me_g + n_group - d, n_group)
            shift = lax.rem((other - me_g) * CAP + width, width)
            total = jnp.where(slot_group == other, roll(dst[d - 1], shift), total)
        return total

    fric_copies = exchange(fric_send, fric_recv, 0)


    def near_traces(rows, store):
        groups, picks = [], []
        for row in rows:
            group = jnp.zeros_like(row)
            for k in range(1, nk):
                group = group + jnp.where(row >= k * elems, 1, 0)
            groups.append(jnp.broadcast_to(group, (fp, elems)))
            picks.append(jnp.broadcast_to(row - group * elems, (fp, elems)))

        def step(f, carry):
            totals = [jnp.zeros((fp, elems), F32) for _ in rows]
            for k in range(nk):
                x = table[f, k * fp : (k + 1) * fp]
                for i, pick in enumerate(picks):
                    got = jnp.take_along_axis(x, pick, axis=1, mode="promise_in_bounds")
                    totals[i] = jnp.where(groups[i] == k, got, totals[i])
            store(f, totals)
            return carry

        lax.fori_loop(0, nf, step, 0, unroll=many)

    def store_rim(f, totals):
        rim_send[f] = totals[0]

    near_traces([roll(rim[...], elems // 2)], store_rim)

    def store_near(f, totals):
        for j in range(1, nj):
            near[j - 1, f] = totals[j - 1]

    first = 2 * (n_group - 1)
    rim_copies = []
    for side, s in enumerate((next_s, prev_s)):
        copy = pltpu.make_async_remote_copy(
            src_ref=rim_send,
            dst_ref=rim_recv.at[side],
            send_sem=send_sem.at[first + side],
            recv_sem=recv_sem.at[first + side],
            device_id=(me_g, s),
            device_id_type=MESH,
        )
        copy.start()
        rim_copies.append(copy)

    near_traces([code[j : j + 1, :] for j in range(1, nj)], store_near)

    state = w_state[0].T[:qp]
    direct = w_state[1].T[:qp]
    rate = 0.5 * jnp.exp(state / direct)
    got = gathered(mean, fric_copies, fric_recv)
    turned = roll(got, slots)
    normal = jnp.where(is_v1, turned, got)
    locked = jnp.where(is_v1, got, turned)
    x = 2.0 - normal
    load = jnp.maximum(x, 0.0) + jnp.log1p(jnp.exp(-jnp.abs(x)))
    strength = load * direct
    magnitude = jnp.abs(locked)
    slip = magnitude / (1.0 + strength * rate)
    for _ in range(1, NEWTON):
        scaled = rate * slip
        root = jnp.sqrt(1.0 + scaled * scaled)
        log = jnp.log(jnp.abs(scaled) + root)
        log = jnp.where(scaled < 0.0, -log, log)
        slip = slip - (slip + strength * log - magnitude) / (1.0 + strength * rate / root)
    signed = jnp.where(locked < 0.0, -slip, jnp.where(locked > 0.0, slip, 0.0))
    slip_send[...] = signed
    slip = jnp.concatenate([slip, jnp.zeros((128 - qp, width), F32)], axis=0)
    evolved = slip.T[:slots, :nq]
    out_state[...] = fault_state[...] + 0.5 * evolution_rate[...] * (
        jnp.exp(-fault_state[...]) - evolved
    )
    slip_copies = exchange(slip_send, slip_recv, n_group - 1)

    for f in range(0, nf, many):
        group = mixed(DERIV % 2, f)
        for m in range(many):
            base[f + m] = group[m]

    for copy in staged:
        copy.wait()

    def face_flux(j, at_row, field):
        def step(i, carry):
            f = i * many
            sums = [None] * many
            for g in range(nf):
                mine, other = own[j, g], field(g)
                for m in range(many):
                    term = own_flux[f + m, g, pl.ds(j, 1), :] * mine
                    term = term + neighbour_flux[f + m, g, pl.ds(j, 1), :] * other
                    sums[m] = term if sums[m] is None else sums[m] + term
            for m in range(many):
                at = pl.ds(pl.multiple_of((f + m) * elems, elems), elems)
                flux[at_row : at_row + fp, at] = sums[m]
            return carry

        lax.fori_loop(0, nf // many, step, 0)

    kj = (nj - 1) * fp
    kr = up(kj, 16)
    for j in range(1, nj):
        face_flux(j, (j - 1) * fp, lambda g, j=j: near[j - 1, g])
    lift_all = w_lift[...].T[:cp]
    lift = roll(lift_all, 128 - fp)
    l_hi, l_lo = halves(lift)
    l_hi, l_lo = l_hi[:, :kr], l_lo[:, :kr]
    k_lane = lax.broadcasted_iota(jnp.int32, lift_all.shape, 1)
    x = flux[:kj]
    high, low = halves(x)
    x_hi = stacked([high], kr)
    r = mul(stacked([l_hi, l_lo], 2 * cp), x_hi)
    r = r[:cp] + r[cp:] + mul(l_hi.astype(BF16), stacked([low], kr))
    for f in range(nf):
        base[f] = base[f] - r[:, f * elems : (f + 1) * elems]

    for copy in rim_copies:
        copy.wait_recv()
    e_lane = lax.broadcasted_iota(jnp.int32, (1, elems), 1)
    has_prev = jnp.where(me_s > 0, 1, 0)
    has_next = jnp.where(me_s < n_sub - 1, 1, 0)
    from_prev = (e_lane < elems // 2) & (has_prev == 1)
    from_next = (e_lane >= elems // 2) & (has_next == 1)
    for f in range(nf):
        near[0, f] = jnp.where(
            from_prev, rim_recv[0, f], jnp.where(from_next, rim_recv[1, f], 0.0)
        )
    face_flux(0, 0, lambda g: near[0, g])
    high, low = halves(flux[:fp])
    l0 = lanes3(jnp.where(k_lane < fp, lift_all, 0.0), fp)[:, : 3 * fp]
    r = mul(l0, stacked([high, high, low], 3 * fp))

    live = jnp.zeros_like(lane)
    for o in range(n_group):
        live = jnp.where(slot_group == o, send_count[0, o], live)
    live = (lane & (CAP - 1)) < live
    side = jnp.where(live, face_row, -1)
    hot0 = jnp.where(is_v1, 0.0, hot)
    hot1 = jnp.where(is_v1, hot, 0.0)
    spread = stacked([hot0, hot1], 2 * elems)
    f_hi, f_lo = halves(w_flift[...])
    kq = 64
    a_lift = jnp.concatenate([f_hi + roll(f_lo, kq), f_hi], axis=1)[:, : 3 * kq].astype(BF16)
    turned = roll(mean, slots)
    locked = jnp.where(is_v1, mean, turned)
    drive_0 = jnp.where(is_v1, 0.5 * (roll(sides, 2 * slots) - sides), locked - sides)
    drive_1 = jnp.where(is_v1, 0.5 * sign_i, -1.0)
    answer = gathered(signed, slip_copies, slip_recv)
    drive = drive_0 + drive_1 * answer
    high, low = halves(drive)
    gap = jnp.zeros((kq - qp, width), F32)
    y = mul(a_lift, stacked([high, gap, high, gap, low, gap], 3 * kq))
    lifted = jnp.where(side == 0, y[:cp], 0.0)
    for k in range(1, nface):
        lifted = jnp.where(side == k, y[k * cp : (k + 1) * cp], lifted)
    high, low = halves(lifted)
    z = lax.dot_general(
        stacked([high, low], 2 * cp),
        spread,
        (((1,), (1,)), ((), ())),
        preferred_element_type=F32,
    )
    z = z[:cp] + z[cp:]
    by_traction, by_jump = z[:, :elems], z[:, elems:]
    for f in range(nf):
        add = coupling[0, f] * by_traction + coupling[1, f] * by_jump
        total = base[f] - r[:, f * elems : (f + 1) * elems] + add
        out[f] = dofs[f] + total[:nb]

    for copy in fric_copies + slip_copies + rim_copies:
        copy.wait_send()


def body(*args):
    args = list(args)
    n_group, n_sub = lax.axis_size("group"), lax.axis_size("sub")
    orders = {1: (1, 2, 0, 3), 3: (1, 0, 2), 5: (1, 2, 0, 3), 6: (1, 2, 0, 3), 7: (2, 0, 1)}
    orders |= {13: (2, 0, 1), 14: (1, 0, 2)}
    orders |= {i: (1, 0) for i in (12, 15, 16, 17, 18)}
    for i, order in orders.items():
        args[i] = jnp.transpose(args[i], order)
    nf, nb, elems = args[0].shape
    nfm, nj, _ = args[3].shape
    nk = args[4].shape[0]
    ndim = args[2].shape[0]
    _, nface, nq = args[13].shape
    slots = args[10].shape[1]
    args[9] = args[9].reshape(1, elems)
    cp, fp, qp = up(nb, 8), up(nfm, 8), up(nq, 8)
    width = 4 * slots
    vmem = pl.BlockSpec(memory_space=pltpu.VMEM)
    smem = pl.BlockSpec(memory_space=pltpu.SMEM)
    specs = [smem if i in (12, 15) else vmem for i in range(len(args))]
    specs[5] = specs[6] = pl.BlockSpec(memory_space=pl.ANY)
    copies = 2 * (n_group - 1) + 2
    dofs, state = pl.pallas_call(
        functools.partial(kernel, n_group, n_sub),
        out_shape=(
            jax.ShapeDtypeStruct(args[0].shape, F32),
            jax.ShapeDtypeStruct(args[16].shape, F32),
        ),
        in_specs=specs,
        out_specs=(vmem, vmem),
        scratch_shapes=[
            pltpu.VMEM((nf, cp, elems), F32),
            pltpu.VMEM((2, nf, ndim * cp, elems), F32),
            pltpu.VMEM((nf, nk * fp, elems), F32),
            pltpu.VMEM((nj, nf, fp, elems), F32),
            pltpu.VMEM((nj, nf, fp, elems), F32),
            pltpu.VMEM((up((nj - 1) * fp, 16), nf * elems), F32),
            pltpu.VMEM((nf, cp, elems), F32),
            pltpu.VMEM((ndim * cp, 128), F32),
            pltpu.VMEM((nj * fp, 128), F32),
            pltpu.VMEM((nk * fp, 128), F32),
            pltpu.VMEM((nface, cp, 128), F32),
            pltpu.VMEM((nface * cp, 128), F32),
            pltpu.VMEM((128, 128), F32),
            pltpu.VMEM((2, width, 128), F32),
            pltpu.VMEM((nf, fp, elems), F32),
            pltpu.VMEM((2, nf, fp, elems), F32),
            pltpu.VMEM((qp, width), F32),
            pltpu.VMEM((n_group - 1, qp, width), F32),
            pltpu.VMEM((qp, width), F32),
            pltpu.VMEM((n_group - 1, qp, width), F32),
            pltpu.VMEM(args[5].shape, F32),
            pltpu.VMEM(args[6].shape, F32),
            pltpu.SemaphoreType.DMA((2,)),
            pltpu.SemaphoreType.DMA((copies,)),
            pltpu.SemaphoreType.DMA((copies,)),
        ],
        compiler_params=pltpu.CompilerParams(collective_id=0, has_side_effects=True),
    )(*args)
    return dofs, state.T


def solution(mesh):
    both = ("group", "sub")
    placed = (
        P(None, None, both),
        P(None, None, None, both),
        P(),
        P(),
        P(),
        P(None, None, None, both),
        P(None, None, None, both),
        P(),
        P(None, both),
        P(both),
        P(None, both),
        P(None, both),
        P(None, both),
        P(),
        P(),
        P(),
        P(None, both),
        P(None, both),
        P(None, both),
    )
    return jax.shard_map(
        body,
        mesh=mesh,
        in_specs=placed,
        out_specs=(P(None, None, both), P(None, both)),
        check_vma=False,
    )
```

profile of v0, /device:TPU:0, one launch (start us, length us, event | category | flops | bytes accessed | tf_op | source)
XLA Modules:
  0.0 19.2 jit_solution(13754979108405333354)
XLA Ops:
  0.6 16.4 %shard_map.194 = (f32[9,35,128]{2,1,0:T(8,128)}, f32[32,49]{1,0:T(8,128)}) custom-call(f32[9,35,128]{2,1,0:T(8,128)} %dofs.1, f32[9,9,3,128]{3,2,1,0:T(4,128)} %bitcast.14, f32[3,35,35]{2,1,0:T(8,128)} %stiff.1, f32[15,4,35]{2,1,0:T(4,128)} %bitcast.19, f32[12,15,35]{2,1,0:T(8,128)} %neighbour_trace.1, f32[9,9,4,128]{3,2,1,0:T(4,128)} %bitcast.15, ...), custom_call_target="tpu_custom_call" | custom-call | tf_op jit(solution)/shard_map/pallas_call | solution.py:465
  17.0 0.0 copy-start
  17.0 1.6 %copy.23 = f32[9,35,128]{2,1,0:T(8,128)} copy(f32[9,35,128]{2,1,0:T(8,128)} %get-tuple-element.8) | data formatting | bytes 322560
  18.6 0.0 copy-done
  18.6 0.6 %copy.24 = f32[49,32]{0,1:T(8,128)} copy(f32[49,32]{0,1:T(8,128)S(1)} %bitcast.24) | data formatting | bytes 12544
Async XLA Ops:
  17.0 1.6 %copy-start = (f32[32,49]{1,0:T(8,128)S(1)}, f32[32,49]{1,0:T(8,128)}, u32[]{:S(2)}) copy-start(f32[32,49]{1,0:T(8,128)} %get-tuple-element.5) | copy-start | bytes 18820
where the time goes:
time: 19.4 us; the launch traced here: 19.2 us
  Pallas kernels  16.4 us (85%)
  local copies, waits for them, and re-layouts  2.22 us (11%)
  between operations  0.66 us (3%)
    pallas_call x1, Pallas kernels, body(): pl.pallas_call(functools.partial(kernel, n_group, n_sub), out_shape=(jax....  16.4 us
    unnamed x4, local copies, waits for them, and re-layouts  2.22 us

commit v1 on v0

--- a/solution.py
+++ b/solution.py
@@ -44,62 +44,94 @@
     return (high + roll(low, step) + roll(high, 2 * step)).astype(BF16)
 
 
-def kernel(
-    n_group,
-    n_sub,
-    dofs,
-    jac,
-    stiff,
-    face_trace,
-    neighbour_trace,
-    own_flux_hbm,
-    neighbour_flux_hbm,
-    face_lift,
-    code,
-    rim,
-    fault_element,
-    fault_face,
-    send_count,
-    fault_trace,
-    fault_lift,
-    coupling,
-    fault_state,
-    direct_effect,
-    evolution_rate,
-    out,
-    out_state,
-    integ,
-    parts,
-    table,
-    own,
-    near,
-    flux,
-    base,
-    w_stiff,
-    w_face,
-    w_near,
-    w_ftrace,
-    w_flift,
-    w_lift,
-    w_state,
-    rim_send,
-    rim_recv,
-    fric_send,
-    fric_recv,
-    slip_send,
-    slip_recv,
-    own_flux,
-    neighbour_flux,
-    stage_sem,
-    send_sem,
-    recv_sem,
-):
-    staged = [
-        pltpu.make_async_copy(own_flux_hbm, own_flux, stage_sem.at[0]),
-        pltpu.make_async_copy(neighbour_flux_hbm, neighbour_flux, stage_sem.at[1]),
-    ]
-    for copy in staged:
-        copy.start()
+def friction(normal, locked, state, direct):
+    rate = 0.5 * jnp.exp(state / direct)
+    x = 2.0 - normal
+    load = jnp.maximum(x, 0.0) + jnp.log1p(jnp.exp(-jnp.abs(x)))
+    strength = load * direct
+    magnitude = jnp.abs(locked)
+    slip = magnitude / (1.0 + strength * rate)
+    for _ in range(1, NEWTON):
+        scaled = rate * slip
+        root = jnp.sqrt(1.0 + scaled * scaled)
+        log = jnp.log(jnp.abs(scaled) + root)
+        log = jnp.where(scaled < 0.0, -log, log)
+        slip = slip - (slip + strength * log - magnitude) / (1.0 + strength * rate / root)
+    return slip
+
+
+N_IN = 19
+ORDER = (2, 0, 1, 10, 13, 16, 17, 4, 3, 9, 8, 7, 11, 14, 18, 12, 15, 5, 6)
+
+
+def kernel(n_group, n_sub, *refs):
+    hbm, out, out_state = refs[:N_IN], refs[N_IN], refs[N_IN + 1]
+    local = refs[N_IN + 2 : 2 * N_IN]
+    (
+        par,
+        integ,
+        parts,
+        table,
+        own,
+        near,
+        flux,
+        base,
+        w_stiff,
+        w_face,
+        w_near,
+        w_ftrace,
+        w_flift,
+        w_lift,
+        rim_send,
+        rim_recv,
+        fric_send,
+        fric_recv,
+        par_recv,
+        slip_pad,
+        stage_sem,
+        send_sem,
+        recv_sem,
+    ) = refs[2 * N_IN :]
+    me_g = lax.axis_index("group")
+    me_s = lax.axis_index("sub")
+    prev_s = lax.rem(me_s + n_sub - 1, n_sub)
+    next_s = lax.rem(me_s + 1, n_sub)
+    barrier = pltpu.get_barrier_semaphore()
+    for d in range(1, n_group):
+        pl.semaphore_signal(
+            barrier, inc=1, device_id=(lax.rem(me_g + d, n_group), me_s), device_id_type=MESH
+        )
+    for s in (prev_s, next_s):
+        pl.semaphore_signal(barrier, inc=1, device_id=(me_g, s), device_id_type=MESH)
+
+    held = list(local[:16]) + [par.at[0], par.at[1]] + list(local[16:])
+    staged = {i: pltpu.make_async_copy(hbm[i], held[i], stage_sem.at[i]) for i in ORDER}
+    for i in ORDER:
+        staged[i].start()
+
+    def arrive(*which):
+        for i in which:
+            staged[i].wait()
+
+    (
+        dofs,
+        jac,
+        stiff,
+        face_trace,
+        neighbour_trace,
+        own_flux,
+        neighbour_flux,
+        face_lift,
+        code,
+        rim,
+        fault_element,
+        fault_face,
+        send_count,
+        fault_trace,
+        fault_lift,
+        coupling,
+    ) = held[:16]
+    evolution_rate = held[18]
     nf, nb, elems = dofs.shape
     ndim = stiff.shape[0]
     nfm, nj, _ = face_trace.shape
@@ -108,51 +140,19 @@
     slots = fault_element.shape[1]
     cp, fp, qp = up(nb, 8), up(nfm, 8), up(nq, 8)
     width = 4 * slots
-    me_g = lax.axis_index("group")
-    me_s = lax.axis_index("sub")
-    prev_s = lax.rem(me_s + n_sub - 1, n_sub)
-    next_s = lax.rem(me_s + 1, n_sub)
-
-    barrier = pltpu.get_barrier_semaphore()
-    for d in range(1, n_group):
-        pl.semaphore_signal(
-            barrier, inc=1, device_id=(lax.rem(me_g + d, n_group), me_s), device_id_type=MESH
-        )
-    for s in (prev_s, next_s):
-        pl.semaphore_signal(barrier, inc=1, device_id=(me_g, s), device_id_type=MESH)
 
     w_stiff[...] = jnp.zeros_like(w_stiff)
+    w_ftrace[...] = jnp.zeros_like(w_ftrace)
     w_face[...] = jnp.zeros_like(w_face)
     w_near[...] = jnp.zeros_like(w_near)
-    w_ftrace[...] = jnp.zeros_like(w_ftrace)
     w_flift[...] = jnp.zeros_like(w_flift)
     w_lift[...] = jnp.zeros_like(w_lift)
+    slip_pad[...] = jnp.zeros_like(slip_pad)
+
+    arrive(2)
     for d in range(ndim):
         w_stiff[d * cp : d * cp + nb, :nb] = stiff[d]
-    for k in range(nface):
-        for b in range(nb):
-            w_ftrace[k, b : b + 1, :nq] = fault_trace[b, pl.ds(k, 1), :]
-            w_flift[k * cp + b : k * cp + b + 1, :nq] = fault_lift[b, pl.ds(k, 1), :]
-    for k in range(nk):
-        w_near[k * fp : k * fp + nfm, :nb] = neighbour_trace[k]
-    for j in range(nj):
-        for q in range(nfm):
-            w_face[j * fp + q : j * fp + q + 1, :nb] = face_trace[q, pl.ds(j, 1), :]
-            w_lift[j * fp + q : j * fp + q + 1, :nb] = face_lift[q, pl.ds(j, 1), :]
-    w_state[0] = jnp.zeros(w_state.shape[1:], F32)
-    w_state[1] = jnp.ones(w_state.shape[1:], F32)
-    for i in range(4):
-        w_state[0, i * slots : (i + 1) * slots, :nq] = fault_state[...]
-        w_state[1, i * slots : (i + 1) * slots, :nq] = direct_effect[...]
-
     a_stiff = lanes3(-w_stiff[...], cp)
-
-    gap = jnp.zeros((128 - cp, 128), F32)
-    v = [jnp.concatenate([w_stiff[d * cp : (d + 1) * cp], gap], axis=0).T[:cp] for d in range(ndim)]
-    a_last = jnp.concatenate(
-        [lanes3(jnp.concatenate(v, axis=0), cp), lanes3(w_near[...], cp), lanes3(w_face[...], cp)],
-        axis=0,
-    )
     many = 3 if nf % 3 == 0 else 1
     rows = ndim * cp
 
@@ -173,6 +173,7 @@
                     sums[m] = term if sums[m] is None else sums[m] + term
         return sums
 
+    arrive(0)
     for f in range(0, nf, many):
         group = [
             jnp.concatenate([dofs[f + m], jnp.zeros((cp - nb, elems), F32)], axis=0)
@@ -183,26 +184,24 @@
             integ[f + m] = group[m]
             parts[0, f + m] = r[:, m * elems : (m + 1) * elems]
 
+    arrive(1)
     factorial = 1.0
     for degree in range(1, DERIV + 1):
         factorial = factorial * (degree + 1)
         turn = (degree - 1) % 2
         for f in range(0, nf, many):
             group = mixed(turn, f)
-            total = [integ[f + m] + group[m] / factorial for m in range(many)]
             for m in range(many):
-                integ[f + m] = total[m]
-            last = degree == DERIV
-            r = mul(a_last if last else a_stiff, spread_out(total if last else group))
-            for m in range(many):
-                y = r[:, m * elems : (m + 1) * elems]
-                parts[1 - turn, f + m] = y[:rows]
-                if last:
-                    table[f + m] = y[rows : rows + nk * fp]
-                    y = y[rows + nk * fp :]
-                    for j in range(nj):
-                        own[j, f + m] = y[j * fp : (j + 1) * fp]
-
+                integ[f + m] = integ[f + m] + group[m] / factorial
+            if degree < DERIV:
+                r = mul(a_stiff, spread_out(group))
+                for m in range(many):
+                    parts[1 - turn, f + m] = r[:, m * elems : (m + 1) * elems]
+
+    arrive(10, 11, 13)
+    for k in range(nface):
+        for b in range(nb):
+            w_ftrace[k, b : b + 1, :nq] = fault_trace[b, pl.ds(k, 1), :]
     lane = lax.broadcasted_iota(jnp.int32, (1, width), 1)
     is_v1 = (lane & slots) != 0
     sign_i = jnp.where((lane & (2 * slots)) != 0, 1.0, -1.0).astype(F32)
@@ -236,38 +235,61 @@
 
     mean = fault_sides(jnp.where(is_v1, 0.5 * g3 + (0.5 * sign_i) * g7, 0.5 * g0))
     mean = mean + roll(mean, 2 * slots)
-    fric_send[...] = mean
+    mean_t = jnp.concatenate([mean, jnp.zeros((128 - qp, width), F32)], axis=0).T
+    normal_here = mean_t[:slots, :nq]
+    locked_here = mean_t[slots : 2 * slots, :nq]
+    fric_send[0] = normal_here
+    fric_send[1] = locked_here
     sides = fault_sides(jnp.where(is_v1, g7, g3))
+    arrive(16, 17)
 
     pl.semaphore_wait(barrier, n_group + 1)
 
-    def exchange(src, dst, first):
-        copies = []
+    here = pl.ds(pl.multiple_of(me_g * CAP, CAP), CAP)
+    par_copies, fric_copies = [], []
+    for src, dst, first, copies in (
+        (par, par_recv, 0, par_copies),
+        (fric_send, fric_recv, n_group - 1, fric_copies),
+    ):
         for d in range(1, n_group):
+            o = lax.rem(me_g + d, n_group)
+            there = pl.ds(pl.multiple_of(o * CAP, CAP), CAP)
             copy = pltpu.make_async_remote_copy(
-                src_ref=src,
-                dst_ref=dst.at[d - 1],
+                src_ref=src.at[:, there, :],
+                dst_ref=dst.at[:, here, :],
                 send_sem=send_sem.at[first + d - 1],
                 recv_sem=recv_sem.at[first + d - 1],
-                device_id=(lax.rem(me_g + d, n_group), me_s),
+                device_id=(o, me_s),
                 device_id_type=MESH,
             )
             copy.start()
             copies.append(copy)
-        return copies
-
-    def gathered(mine, copies, dst):
-        total = jnp.where(slot_group == me_g, mine, 0.0)
-        for d, copy in enumerate(copies, 1):
-            copy.wait_recv()
-            other = lax.rem(me_g + n_group - d, n_group)
-            shift = lax.rem((other - me_g) * CAP + width, width)
-            total = jnp.where(slot_group == other, roll(dst[d - 1], shift), total)
-        return total
-
-    fric_copies = exchange(fric_send, fric_recv, 0)
-
-
+        dst[:, here, :] = src[:, here, :]
+
+    arrive(3, 4)
+    for k in range(nk):
+        w_near[k * fp : k * fp + nfm, :nb] = neighbour_trace[k]
+    for j in range(nj):
+        for q in range(nfm):
+            w_face[j * fp + q : j * fp + q + 1, :nb] = face_trace[q, pl.ds(j, 1), :]
+    gap = jnp.zeros((128 - cp, 128), F32)
+    v = [jnp.concatenate([w_stiff[d * cp : (d + 1) * cp], gap], axis=0).T[:cp] for d in range(ndim)]
+    a_last = jnp.concatenate(
+        [lanes3(jnp.concatenate(v, axis=0), cp), lanes3(w_near[...], cp), lanes3(w_face[...], cp)],
+        axis=0,
+    )
+    turn = DERIV % 2
+    for f in range(0, nf, many):
+        r = mul(a_last, spread_out([integ[f + m] for m in range(many)]))
+        for m in range(many):
+            y = r[:, m * elems : (m + 1) * elems]
+            parts[turn, f + m] = y[:rows]
+            table[f + m] = y[rows : rows + nk * fp]
+            y = y[rows + nk * fp :]
+            for j in range(nj):
+                own[j, f + m] = y[j * fp : (j + 1) * fp]
+
+    arrive(8, 9)
     def near_traces(rows, store):
         groups, picks = [], []
         for row in rows:
@@ -314,41 +336,15 @@
 
     near_traces([code[j : j + 1, :] for j in range(1, nj)], store_near)
 
-    state = w_state[0].T[:qp]
-    direct = w_state[1].T[:qp]
-    rate = 0.5 * jnp.exp(state / direct)
-    got = gathered(mean, fric_copies, fric_recv)
-    turned = roll(got, slots)
-    normal = jnp.where(is_v1, turned, got)
-    locked = jnp.where(is_v1, got, turned)
-    x = 2.0 - normal
-    load = jnp.maximum(x, 0.0) + jnp.log1p(jnp.exp(-jnp.abs(x)))
-    strength = load * direct
-    magnitude = jnp.abs(locked)
-    slip = magnitude / (1.0 + strength * rate)
-    for _ in range(1, NEWTON):
-        scaled = rate * slip
-        root = jnp.sqrt(1.0 + scaled * scaled)
-        log = jnp.log(jnp.abs(scaled) + root)
-        log = jnp.where(scaled < 0.0, -log, log)
-        slip = slip - (slip + strength * log - magnitude) / (1.0 + strength * rate / root)
-    signed = jnp.where(locked < 0.0, -slip, jnp.where(locked > 0.0, slip, 0.0))
-    slip_send[...] = signed
-    slip = jnp.concatenate([slip, jnp.zeros((128 - qp, width), F32)], axis=0)
-    evolved = slip.T[:slots, :nq]
-    out_state[...] = fault_state[...] + 0.5 * evolution_rate[...] * (
-        jnp.exp(-fault_state[...]) - evolved
-    )
-    slip_copies = exchange(slip_send, slip_recv, n_group - 1)
-
     for f in range(0, nf, many):
-        group = mixed(DERIV % 2, f)
+        group = mixed(turn, f)
         for m in range(many):
             base[f + m] = group[m]
 
-    for copy in staged:
-        copy.wait()
-
+    arrive(5, 6, 7)
+    for j in range(nj):
+        for q in range(nfm):
+            w_lift[j * fp + q : j * fp + q + 1, :nb] = face_lift[q, pl.ds(j, 1), :]
     def face_flux(j, at_row, field):
         def step(i, carry):
             f = i * many
@@ -383,22 +379,17 @@
     for f in range(nf):
         base[f] = base[f] - r[:, f * elems : (f + 1) * elems]
 
-    for copy in rim_copies:
+    for copy in par_copies:
         copy.wait_recv()
-    e_lane = lax.broadcasted_iota(jnp.int32, (1, elems), 1)
-    has_prev = jnp.where(me_s > 0, 1, 0)
-    has_next = jnp.where(me_s < n_sub - 1, 1, 0)
-    from_prev = (e_lane < elems // 2) & (has_prev == 1)
-    from_next = (e_lane >= elems // 2) & (has_next == 1)
-    for f in range(nf):
-        near[0, f] = jnp.where(
-            from_prev, rim_recv[0, f], jnp.where(from_next, rim_recv[1, f], 0.0)
-        )
-    face_flux(0, 0, lambda g: near[0, g])
-    high, low = halves(flux[:fp])
-    l0 = lanes3(jnp.where(k_lane < fp, lift_all, 0.0), fp)[:, : 3 * fp]
-    r = mul(l0, stacked([high, high, low], 3 * fp))
-
+    slip = friction(normal_here, locked_here, par_recv[0], par_recv[1])
+    signed = jnp.where(locked_here < 0.0, -slip, jnp.where(locked_here > 0.0, slip, 0.0))
+    for i in range(4):
+        slip_pad[i * slots : (i + 1) * slots, :nq] = signed
+
+    arrive(12, 14, 15)
+    for k in range(nface):
+        for b in range(nb):
+            w_flift[k * cp + b : k * cp + b + 1, :nq] = fault_lift[b, pl.ds(k, 1), :]
     live = jnp.zeros_like(lane)
     for o in range(n_group):
         live = jnp.where(slot_group == o, send_count[0, o], live)
@@ -414,7 +405,7 @@
     locked = jnp.where(is_v1, mean, turned)
     drive_0 = jnp.where(is_v1, 0.5 * (roll(sides, 2 * slots) - sides), locked - sides)
     drive_1 = jnp.where(is_v1, 0.5 * sign_i, -1.0)
-    answer = gathered(signed, slip_copies, slip_recv)
+    answer = slip_pad[...].T[:qp]
     drive = drive_0 + drive_1 * answer
     high, low = halves(drive)
     gap = jnp.zeros((kq - qp, width), F32)
@@ -431,13 +422,48 @@
     )
     z = z[:cp] + z[cp:]
     by_traction, by_jump = z[:, :elems], z[:, elems:]
+    for copy in rim_copies:
+        copy.wait_recv()
+    e_lane = lax.broadcasted_iota(jnp.int32, (1, elems), 1)
+    has_prev = jnp.where(me_s > 0, 1, 0)
+    has_next = jnp.where(me_s < n_sub - 1, 1, 0)
+    from_prev = (e_lane < elems // 2) & (has_prev == 1)
+    from_next = (e_lane >= elems // 2) & (has_next == 1)
+    for f in range(nf):
+        near[0, f] = jnp.where(
+            from_prev, rim_recv[0, f], jnp.where(from_next, rim_recv[1, f], 0.0)
+        )
+    face_flux(0, 0, lambda g: near[0, g])
+    high, low = halves(flux[:fp])
+    l0 = lanes3(jnp.where(k_lane < fp, lift_all, 0.0), fp)[:, : 3 * fp]
+    r = mul(l0, stacked([high, high, low], 3 * fp))
+
     for f in range(nf):
         add = coupling[0, f] * by_traction + coupling[1, f] * by_jump
         total = base[f] - r[:, f * elems : (f + 1) * elems] + add
         out[f] = dofs[f] + total[:nb]
 
-    for copy in fric_copies + slip_copies + rim_copies:
+
+    arrive(18)
+    for copy in fric_copies:
+        copy.wait_recv()
+    state = par[0]
+    slip = friction(fric_recv[0], fric_recv[1], state, par[1])
+    out_state[...] = state + 0.5 * evolution_rate[...] * (jnp.exp(-state) - slip)
+
+    for copy in par_copies + fric_copies + rim_copies:
         copy.wait_send()
+
+
+def finish(dofs, state, out, out_state, sem):
+    copies = [
+        pltpu.make_async_copy(dofs, out, sem.at[0]),
+        pltpu.make_async_copy(state, out_state, sem.at[1]),
+    ]
+    for copy in copies:
+        copy.start()
+    for copy in copies:
+        copy.wait()
 
 
 def body(*args):
@@ -458,19 +484,19 @@
     cp, fp, qp = up(nb, 8), up(nfm, 8), up(nq, 8)
     width = 4 * slots
     vmem = pl.BlockSpec(memory_space=pltpu.VMEM)
-    smem = pl.BlockSpec(memory_space=pltpu.SMEM)
-    specs = [smem if i in (12, 15) else vmem for i in range(len(args))]
-    specs[5] = specs[6] = pl.BlockSpec(memory_space=pl.ANY)
+    anywhere = pl.BlockSpec(memory_space=pl.ANY)
+    held = [(pltpu.SMEM if i in (12, 15) else pltpu.VMEM)(a.shape, a.dtype) for i, a in enumerate(args)]
+    shapes = (args[0].shape, args[16].shape)
     copies = 2 * (n_group - 1) + 2
     dofs, state = pl.pallas_call(
         functools.partial(kernel, n_group, n_sub),
-        out_shape=(
-            jax.ShapeDtypeStruct(args[0].shape, F32),
-            jax.ShapeDtypeStruct(args[16].shape, F32),
-        ),
-        in_specs=specs,
+        out_shape=tuple(pltpu.VMEM(s, F32) for s in shapes),
+        in_specs=[anywhere] * len(args),
         out_specs=(vmem, vmem),
-        scratch_shapes=[
+        scratch_shapes=held[:16]
+        + held[18:]
+        + [
+            pltpu.VMEM((2,) + args[16].shape, F32),
             pltpu.VMEM((nf, cp, elems), F32),
             pltpu.VMEM((2, nf, ndim * cp, elems), F32),
             pltpu.VMEM((nf, nk * fp, elems), F32),
@@ -484,21 +510,26 @@
             pltpu.VMEM((nface, cp, 128), F32),
             pltpu.VMEM((nface * cp, 128), F32),
             pltpu.VMEM((128, 128), F32),
-            pltpu.VMEM((2, width, 128), F32),
             pltpu.VMEM((nf, fp, elems), F32),
             pltpu.VMEM((2, nf, fp, elems), F32),
-            pltpu.VMEM((qp, width), F32),
-            pltpu.VMEM((n_group - 1, qp, width), F32),
-            pltpu.VMEM((qp, width), F32),
-            pltpu.VMEM((n_group - 1, qp, width), F32),
-            pltpu.VMEM(args[5].shape, F32),
-            pltpu.VMEM(args[6].shape, F32),
-            pltpu.SemaphoreType.DMA((2,)),
+            pltpu.VMEM((2, slots, nq), F32),
+            pltpu.VMEM((2, slots, nq), F32),
+            pltpu.VMEM((2, slots, nq), F32),
+            pltpu.VMEM((width, 128), F32),
+            pltpu.SemaphoreType.DMA((len(args),)),
             pltpu.SemaphoreType.DMA((copies,)),
             pltpu.SemaphoreType.DMA((copies,)),
         ],
         compiler_params=pltpu.CompilerParams(collective_id=0, has_side_effects=True),
     )(*args)
+    dofs, state = pl.pallas_call(
+        finish,
+        out_shape=tuple(jax.ShapeDtypeStruct(s, F32) for s in shapes),
+        in_specs=[vmem, vmem],
+        out_specs=(anywhere, anywhere),
+        scratch_shapes=[pltpu.SemaphoreType.DMA((2,))],
+        compiler_params=pltpu.CompilerParams(vmem_limit_bytes=8 << 20),
+    )(dofs, state)
     return dofs, state.T
 
 

time: 19.4 us -> 13.2 us (0.68)
  Pallas kernels: 16.4 us -> 12.4 us
  local copies, waits for them, and re-layouts: 2.22 us -> 0 us
    pallas_call x1 -> x2, Pallas kernels: 16.4 us -> 12.4 us  [the longest x1 11.7 us: body(): pl.pallas_call(functools.partial(kernel, n_group, n_sub), out_shape=tuple...]
    unnamed x4 -> x0, local copies, waits for them, and re-layouts: 2.22 us -> none
where the time goes in v1:
time: 13.2 us; the launch traced here: 13 us
  Pallas kernels  12.4 us (94%)
  between operations  0.65 us (5%)
    pallas_call x1, Pallas kernels, body(): pl.pallas_call(functools.partial(kernel, n_group, n_sub), out_shape=tuple...  11.7 us
    pallas_call x1, Pallas kernels, body(): pl.pallas_call(finish, out_shape=tuple((jax.ShapeDtypeStruct(s, F32) for...  0.69 us

profile of v1, /device:TPU:0, one launch (start us, length us, event | category | flops | bytes accessed | tf_op | source)
XLA Modules:
  0.0 13.0 jit_solution(16185481841914376031)
XLA Ops:
  0.6 11.7 %shard_map.194 = (f32[9,35,128]{2,1,0:T(8,128)S(1)}, f32[32,49]{1,0:T(8,128)S(1)}) custom-call(f32[9,35,128]{2,1,0:T(8,128)} %refs_0_.1, f32[9,9,3,128]{3,2,1,0:T(4,128)} %bitcast.14, f32[3,35,35]{2,1,0:T(8,128)} %refs_2_.1, f32[15,4,35]{2,1,0:T(4,128)} %bitcast.19, f32[12,15,35]{2,1,0:T(8,128)} %refs_4_.1, f32[9,9,4,128]{3,2,1,0:T(4,128)} %bitcast.15, ...), custom_call_target="tpu_custom_call" | custom-call | tf_op jit(solution)/shard_map/pallas_call | solution.py:491
  12.3 0.7 %shard_map.195 = (f32[9,35,128]{2,1,0:T(8,128)}, f32[32,49]{1,0:T(8,128)}) custom-call(f32[9,35,128]{2,1,0:T(8,128)S(1)} %get-tuple-element.6.dofs, f32[32,49]{1,0:T(8,128)S(1)} %get-tuple-element.7.state), custom_call_target="tpu_custom_call" | custom-call | tf_op jit(solution)/shard_map/pallas_call | solution.py:525

commit v2 on v1

--- a/solution.py
+++ b/solution.py
@@ -71,7 +71,7 @@
         par,
         integ,
         parts,
-        table,
+        gathered,
         own,
         near,
         flux,
@@ -149,6 +149,46 @@
     w_lift[...] = jnp.zeros_like(w_lift)
     slip_pad[...] = jnp.zeros_like(slip_pad)
 
+    here = pl.ds(pl.multiple_of(me_g * CAP, CAP), CAP)
+
+    def to_group(src, dst, first):
+        copies = []
+        for d in range(1, n_group):
+            o = lax.rem(me_g + d, n_group)
+            there = pl.ds(pl.multiple_of(o * CAP, CAP), CAP)
+            copies.append(
+                pltpu.make_async_remote_copy(
+                    src_ref=src.at[:, there, :],
+                    dst_ref=dst.at[:, here, :],
+                    send_sem=send_sem.at[first + d - 1],
+                    recv_sem=recv_sem.at[first + d - 1],
+                    device_id=(o, me_s),
+                    device_id_type=MESH,
+                )
+            )
+        return copies
+
+    par_copies = to_group(par, par_recv, 0)
+    fric_copies = to_group(fric_send, fric_recv, n_group - 1)
+    rim_copies = []
+    for side, s in enumerate((next_s, prev_s)):
+        rim_copies.append(
+            pltpu.make_async_remote_copy(
+                src_ref=rim_send,
+                dst_ref=rim_recv.at[side],
+                send_sem=send_sem.at[2 * (n_group - 1) + side],
+                recv_sem=recv_sem.at[2 * (n_group - 1) + side],
+                device_id=(me_g, s),
+                device_id_type=MESH,
+            )
+        )
+
+    def begin(copies):
+        for copy in copies:
+            copy.start()
+
+    early = me_g > 0
+
     arrive(2)
     for d in range(ndim):
         w_stiff[d * cp : d * cp + nb, :nb] = stiff[d]
@@ -197,6 +237,14 @@
                 r = mul(a_stiff, spread_out(group))
                 for m in range(many):
                     parts[1 - turn, f + m] = r[:, m * elems : (m + 1) * elems]
+        if degree == 2:
+            arrive(16, 17)
+            par_recv[:, here, :] = par[:, here, :]
+
+            @pl.when(early)
+            def _():
+                pl.semaphore_wait(barrier, n_group + 1)
+                begin(par_copies)
 
     arrive(10, 11, 13)
     for k in range(nface):
@@ -241,30 +289,11 @@
     fric_send[0] = normal_here
     fric_send[1] = locked_here
     sides = fault_sides(jnp.where(is_v1, g7, g3))
-    arrive(16, 17)
-
-    pl.semaphore_wait(barrier, n_group + 1)
-
-    here = pl.ds(pl.multiple_of(me_g * CAP, CAP), CAP)
-    par_copies, fric_copies = [], []
-    for src, dst, first, copies in (
-        (par, par_recv, 0, par_copies),
-        (fric_send, fric_recv, n_group - 1, fric_copies),
-    ):
-        for d in range(1, n_group):
-            o = lax.rem(me_g + d, n_group)
-            there = pl.ds(pl.multiple_of(o * CAP, CAP), CAP)
-            copy = pltpu.make_async_remote_copy(
-                src_ref=src.at[:, there, :],
-                dst_ref=dst.at[:, here, :],
-                send_sem=send_sem.at[first + d - 1],
-                recv_sem=recv_sem.at[first + d - 1],
-                device_id=(o, me_s),
-                device_id_type=MESH,
-            )
-            copy.start()
-            copies.append(copy)
-        dst[:, here, :] = src[:, here, :]
+    fric_recv[:, here, :] = fric_send[:, here, :]
+
+    @pl.when(early)
+    def _():
+        begin(fric_copies)
 
     arrive(3, 4)
     for k in range(nk):
@@ -275,71 +304,78 @@
     gap = jnp.zeros((128 - cp, 128), F32)
     v = [jnp.concatenate([w_stiff[d * cp : (d + 1) * cp], gap], axis=0).T[:cp] for d in range(ndim)]
     a_last = jnp.concatenate(
-        [lanes3(jnp.concatenate(v, axis=0), cp), lanes3(w_near[...], cp), lanes3(w_face[...], cp)],
-        axis=0,
+        [lanes3(jnp.concatenate(v, axis=0), cp), lanes3(w_face[...], cp)], axis=0
     )
+    a_near = lanes3(w_near[...], cp)
     turn = DERIV % 2
     for f in range(0, nf, many):
         r = mul(a_last, spread_out([integ[f + m] for m in range(many)]))
         for m in range(many):
             y = r[:, m * elems : (m + 1) * elems]
             parts[turn, f + m] = y[:rows]
-            table[f + m] = y[rows : rows + nk * fp]
-            y = y[rows + nk * fp :]
+            y = y[rows:]
             for j in range(nj):
                 own[j, f + m] = y[j * fp : (j + 1) * fp]
 
     arrive(8, 9)
-    def near_traces(rows, store):
-        groups, picks = [], []
-        for row in rows:
-            group = jnp.zeros_like(row)
-            for k in range(1, nk):
-                group = group + jnp.where(row >= k * elems, 1, 0)
-            groups.append(jnp.broadcast_to(group, (fp, elems)))
-            picks.append(jnp.broadcast_to(row - group * elems, (fp, elems)))
-
-        def step(f, carry):
-            totals = [jnp.zeros((fp, elems), F32) for _ in rows]
-            for k in range(nk):
-                x = table[f, k * fp : (k + 1) * fp]
-                for i, pick in enumerate(picks):
-                    got = jnp.take_along_axis(x, pick, axis=1, mode="promise_in_bounds")
-                    totals[i] = jnp.where(groups[i] == k, got, totals[i])
-            store(f, totals)
-            return carry
-
-        lax.fori_loop(0, nf, step, 0, unroll=many)
-
-    def store_rim(f, totals):
-        rim_send[f] = totals[0]
-
-    near_traces([roll(rim[...], elems // 2)], store_rim)
-
-    def store_near(f, totals):
-        for j in range(1, nj):
-            near[j - 1, f] = totals[j - 1]
-
-    first = 2 * (n_group - 1)
-    rim_copies = []
-    for side, s in enumerate((next_s, prev_s)):
-        copy = pltpu.make_async_remote_copy(
-            src_ref=rim_send,
-            dst_ref=rim_recv.at[side],
-            send_sem=send_sem.at[first + side],
-            recv_sem=recv_sem.at[first + side],
-            device_id=(me_g, s),
-            device_id_type=MESH,
-        )
-        copy.start()
-        rim_copies.append(copy)
-
-    near_traces([code[j : j + 1, :] for j in range(1, nj)], store_near)
+    picked = [roll(rim[...], elems // 2)] + [code[j : j + 1, :] for j in range(1, nj)]
+    maps, hots = [], []
+    for row in picked:
+        group = jnp.zeros_like(row)
+        for k in range(1, nk):
+            group = group + jnp.where(row >= k * elems, 1, 0)
+        maps.append(group)
+        hit = lax.broadcasted_iota(jnp.int32, (elems, elems), 0) == row - group * elems
+        hots.append(jnp.where(hit, 1.0, 0.0).astype(F32))
+    column = jnp.concatenate(hots, axis=1).astype(BF16)
+    whole = jnp.concatenate([integ[f] for f in range(nf)], axis=0)
+    high, low = halves(whole)
+    tall = up(nf * cp, 16)
+    gathered[...] = mul(
+        jnp.concatenate([stacked([high], tall), stacked([low], tall)], axis=1),
+        jnp.concatenate([column, column], axis=0),
+    )
+
+    def near_traces(i, store):
+        which = jnp.broadcast_to(maps[i], (fp, elems))
+        for f in range(0, nf, many):
+            at = slice(i * elems, (i + 1) * elems)
+            r = mul(
+                a_near,
+                spread_out([gathered[(f + m) * cp : (f + m + 1) * cp, at] for m in range(many)]),
+            )
+            for m in range(many):
+                y = r[:, m * elems : (m + 1) * elems]
+                total = y[:fp]
+                for k in range(1, nk):
+                    total = jnp.where(which == k, y[k * fp : (k + 1) * fp], total)
+                store(f + m, total)
+
+    def store_rim(f, total):
+        rim_send[f] = total
+
+    near_traces(0, store_rim)
+
+    @pl.when(early)
+    def _():
+        begin(rim_copies)
+
+    for j in range(1, nj):
+
+        def store_near(f, total, j=j):
+            near[j - 1, f] = total
+
+        near_traces(j, store_near)
 
     for f in range(0, nf, many):
         group = mixed(turn, f)
         for m in range(many):
             base[f + m] = group[m]
+
+    @pl.when(jnp.logical_not(early))
+    def _():
+        pl.semaphore_wait(barrier, n_group + 1)
+        begin(par_copies + fric_copies + rim_copies)
 
     arrive(5, 6, 7)
     for j in range(nj):
@@ -499,7 +535,7 @@
             pltpu.VMEM((2,) + args[16].shape, F32),
             pltpu.VMEM((nf, cp, elems), F32),
             pltpu.VMEM((2, nf, ndim * cp, elems), F32),
-            pltpu.VMEM((nf, nk * fp, elems), F32),
+            pltpu.VMEM((up(nf * cp, 16), nj * elems), F32),
             pltpu.VMEM((nj, nf, fp, elems), F32),
             pltpu.VMEM((nj, nf, fp, elems), F32),
             pltpu.VMEM((up((nj - 1) * fp, 16), nf * elems), F32),

time: 13.2 us -> 13.2 us (level)
  no operation moved by 1% of the time
where the time goes in v2:
time: 13.2 us; the launch traced here: 13 us
  Pallas kernels  12.4 us (94%)
  between operations  0.65 us (5%)
    pallas_call x1, Pallas kernels, body(): pl.pallas_call(functools.partial(kernel, n_group, n_sub), out_shape=tuple...  11.7 us
    pallas_call x1, Pallas kernels, body(): pl.pallas_call(finish, out_shape=tuple((jax.ShapeDtypeStruct(s, F32) for...  0.69 us

profile of v2, /device:TPU:0, one launch (start us, length us, event | category | flops | bytes accessed | tf_op | source)
XLA Modules:
  0.0 13.0 jit_solution(13133334966816344919)
XLA Ops:
  0.6 11.7 %shard_map.194 = (f32[9,35,128]{2,1,0:T(8,128)S(1)}, f32[32,49]{1,0:T(8,128)S(1)}) custom-call(f32[9,35,128]{2,1,0:T(8,128)} %refs_0_.1, f32[9,9,3,128]{3,2,1,0:T(4,128)} %bitcast.14, f32[3,35,35]{2,1,0:T(8,128)} %refs_2_.1, f32[15,4,35]{2,1,0:T(4,128)} %bitcast.19, f32[12,15,35]{2,1,0:T(8,128)} %refs_4_.1, f32[9,9,4,128]{3,2,1,0:T(4,128)} %bitcast.15, ...), custom_call_target="tpu_custom_call" | custom-call | tf_op jit(solution)/shard_map/pallas_call | solution.py:527
  12.3 0.7 %shard_map.195 = (f32[9,35,128]{2,1,0:T(8,128)}, f32[32,49]{1,0:T(8,128)}) custom-call(f32[9,35,128]{2,1,0:T(8,128)S(1)} %get-tuple-element.6.dofs, f32[32,49]{1,0:T(8,128)S(1)} %get-tuple-element.7.state), custom_call_target="tpu_custom_call" | custom-call | tf_op jit(solution)/shard_map/pallas_call | solution.py:561

commit v3 on v2

--- a/solution.py
+++ b/solution.py
@@ -61,7 +61,7 @@
 
 
 N_IN = 19
-ORDER = (2, 0, 1, 10, 13, 16, 17, 4, 3, 9, 8, 7, 11, 14, 18, 12, 15, 5, 6)
+ORDER = (2, 0, 1, 13, 10, 11, 16, 17, 4, 3, 9, 8, 7, 14, 18, 12, 15, 5, 6)
 
 
 def kernel(n_group, n_sub, *refs):
@@ -86,23 +86,28 @@
         rim_recv,
         fric_send,
         fric_recv,
+        par_send,
         par_recv,
-        slip_pad,
         stage_sem,
         send_sem,
         recv_sem,
     ) = refs[2 * N_IN :]
     me_g = lax.axis_index("group")
     me_s = lax.axis_index("sub")
-    prev_s = lax.rem(me_s + n_sub - 1, n_sub)
-    next_s = lax.rem(me_s + 1, n_sub)
+    has_prev = me_s > 0
+    has_next = me_s < n_sub - 1
     barrier = pltpu.get_barrier_semaphore()
     for d in range(1, n_group):
         pl.semaphore_signal(
             barrier, inc=1, device_id=(lax.rem(me_g + d, n_group), me_s), device_id_type=MESH
         )
-    for s in (prev_s, next_s):
-        pl.semaphore_signal(barrier, inc=1, device_id=(me_g, s), device_id_type=MESH)
+    for side, s in ((has_prev, me_s - 1), (has_next, me_s + 1)):
+
+        @pl.when(side)
+        def _(s=s):
+            pl.semaphore_signal(barrier, inc=1, device_id=(me_g, s), device_id_type=MESH)
+
+    greeted = n_group - 1 + jnp.where(has_prev, 1, 0) + jnp.where(has_next, 1, 0)
 
     held = list(local[:16]) + [par.at[0], par.at[1]] + list(local[16:])
     staged = {i: pltpu.make_async_copy(hbm[i], held[i], stage_sem.at[i]) for i in ORDER}
@@ -147,19 +152,16 @@
     w_near[...] = jnp.zeros_like(w_near)
     w_flift[...] = jnp.zeros_like(w_flift)
     w_lift[...] = jnp.zeros_like(w_lift)
-    slip_pad[...] = jnp.zeros_like(slip_pad)
-
-    here = pl.ds(pl.multiple_of(me_g * CAP, CAP), CAP)
+    par_send[...] = jnp.ones_like(par_send)
 
     def to_group(src, dst, first):
         copies = []
         for d in range(1, n_group):
             o = lax.rem(me_g + d, n_group)
-            there = pl.ds(pl.multiple_of(o * CAP, CAP), CAP)
             copies.append(
                 pltpu.make_async_remote_copy(
-                    src_ref=src.at[:, there, :],
-                    dst_ref=dst.at[:, here, :],
+                    src_ref=src.at[o],
+                    dst_ref=dst.at[me_g],
                     send_sem=send_sem.at[first + d - 1],
                     recv_sem=recv_sem.at[first + d - 1],
                     device_id=(o, me_s),
@@ -168,13 +170,13 @@
             )
         return copies
 
-    par_copies = to_group(par, par_recv, 0)
+    par_copies = to_group(par_send, par_recv, 0)
     fric_copies = to_group(fric_send, fric_recv, n_group - 1)
     rim_copies = []
-    for side, s in enumerate((next_s, prev_s)):
+    for side, s in enumerate((me_s + 1, me_s - 1)):
         rim_copies.append(
             pltpu.make_async_remote_copy(
-                src_ref=rim_send,
+                src_ref=rim_send.at[side],
                 dst_ref=rim_recv.at[side],
                 send_sem=send_sem.at[2 * (n_group - 1) + side],
                 recv_sem=recv_sem.at[2 * (n_group - 1) + side],
@@ -187,7 +189,12 @@
         for copy in copies:
             copy.start()
 
-    early = me_g > 0
+    def begin_rim():
+        for copy, there in zip(rim_copies, (has_next, has_prev)):
+            pl.when(there)(copy.start)
+
+    first_row = me_g == 0
+    corner = first_row & (me_s == 0)
 
     arrive(2)
     for d in range(ndim):
@@ -203,13 +210,13 @@
             out.append(stacked([high, high, low], 128))
         return jnp.concatenate(out, axis=1)
 
-    def mixed(turn, f):
-        sums = [None] * many
+    def mixed(turn, fields):
+        sums = [None] * len(fields)
         for g in range(nf):
             for d in range(ndim):
                 x = parts[turn, g, d * cp : (d + 1) * cp]
-                for m in range(many):
-                    term = jac[f + m, g, pl.ds(d, 1), :] * x
+                for m, f in enumerate(fields):
+                    term = jac[f, g, pl.ds(d, 1), :] * x
                     sums[m] = term if sums[m] is None else sums[m] + term
         return sums
 
@@ -225,27 +232,6 @@
             parts[0, f + m] = r[:, m * elems : (m + 1) * elems]
 
     arrive(1)
-    factorial = 1.0
-    for degree in range(1, DERIV + 1):
-        factorial = factorial * (degree + 1)
-        turn = (degree - 1) % 2
-        for f in range(0, nf, many):
-            group = mixed(turn, f)
-            for m in range(many):
-                integ[f + m] = integ[f + m] + group[m] / factorial
-            if degree < DERIV:
-                r = mul(a_stiff, spread_out(group))
-                for m in range(many):
-                    parts[1 - turn, f + m] = r[:, m * elems : (m + 1) * elems]
-        if degree == 2:
-            arrive(16, 17)
-            par_recv[:, here, :] = par[:, here, :]
-
-            @pl.when(early)
-            def _():
-                pl.semaphore_wait(barrier, n_group + 1)
-                begin(par_copies)
-
     arrive(10, 11, 13)
     for k in range(nface):
         for b in range(nb):
@@ -261,11 +247,6 @@
     hit = lax.broadcasted_iota(jnp.int32, (elems, width), 0) == elem_row
     hot = jnp.where(hit, 1.0, 0.0).astype(F32)
 
-    i0, i3, i7 = integ[0], integ[3], integ[7]
-    highs, lows = zip(*[halves(x) for x in (i0, i3, i7)])
-    g = mul(stacked(list(highs) + list(lows), 6 * cp), hot.astype(BF16))
-    g = g[: 3 * cp] + g[3 * cp :]
-    g0, g3, g7 = g[:cp], g[cp : 2 * cp], g[2 * cp :]
     a_fault = []
     for k in range(nface):
         high, low = halves(w_ftrace[k])
@@ -273,6 +254,43 @@
         a_fault.append(jnp.concatenate([high, low, high, gap], axis=0).T[:qp])
     a_fault = jnp.concatenate(a_fault, axis=0).astype(BF16)
 
+    factorial = 1.0
+    for degree in range(1, DERIV):
+        factorial = factorial * (degree + 1)
+        turn = (degree - 1) % 2
+        for f in range(0, nf, many):
+            group = mixed(turn, range(f, f + many))
+            for m in range(many):
+                integ[f + m] = integ[f + m] + group[m] / factorial
+            r = mul(a_stiff, spread_out(group))
+            for m in range(many):
+                parts[1 - turn, f + m] = r[:, m * elems : (m + 1) * elems]
+        if degree == 2:
+            arrive(16, 17)
+            for o in range(n_group):
+                for i in range(2):
+                    par_send[o, i, :, :nq] = par[i, o * CAP : (o + 1) * CAP, :]
+            par_recv[me_g] = par_send[me_g]
+
+            @pl.when(jnp.logical_not(first_row))
+            def _():
+                pl.semaphore_wait(barrier, greeted)
+                begin(par_copies)
+
+    factorial = factorial * (DERIV + 1)
+
+    def finished(fields):
+        for f, x in zip(fields, mixed((DERIV - 1) % 2, fields)):
+            integ[f] = integ[f] + x / factorial
+
+    picked = (0, 3, 7)
+    finished(picked)
+
+    i0, i3, i7 = integ[0], integ[3], integ[7]
+    highs, lows = zip(*[halves(x) for x in (i0, i3, i7)])
+    g = mul(stacked(list(highs) + list(lows), 6 * cp), hot.astype(BF16))
+    g = g[: 3 * cp] + g[3 * cp :]
+    g0, g3, g7 = g[:cp], g[cp : 2 * cp], g[2 * cp :]
     def fault_sides(x):
         high, low = halves(x)
         y = mul(a_fault, stacked([high, high, low], 128))
@@ -284,16 +302,26 @@
     mean = fault_sides(jnp.where(is_v1, 0.5 * g3 + (0.5 * sign_i) * g7, 0.5 * g0))
     mean = mean + roll(mean, 2 * slots)
     mean_t = jnp.concatenate([mean, jnp.zeros((128 - qp, width), F32)], axis=0).T
-    normal_here = mean_t[:slots, :nq]
-    locked_here = mean_t[slots : 2 * slots, :nq]
-    fric_send[0] = normal_here
-    fric_send[1] = locked_here
-    sides = fault_sides(jnp.where(is_v1, g7, g3))
-    fric_recv[:, here, :] = fric_send[:, here, :]
-
-    @pl.when(early)
+    normal_here = mean_t[:slots]
+    locked_here = mean_t[slots : 2 * slots]
+    for o in range(n_group):
+        fric_send[o, 0] = normal_here[o * CAP : (o + 1) * CAP]
+        fric_send[o, 1] = locked_here[o * CAP : (o + 1) * CAP]
+    fric_recv[me_g] = fric_send[me_g]
+
+    @pl.when(jnp.logical_not(first_row))
     def _():
         begin(fric_copies)
+
+    @pl.when(first_row & (me_s > 0))
+    def _():
+        pl.semaphore_wait(barrier, greeted)
+        begin(par_copies + fric_copies)
+
+    sides = fault_sides(jnp.where(is_v1, g7, g3))
+    rest = [f for f in range(nf) if f not in picked]
+    for i in range(0, len(rest), many):
+        finished(rest[i : i + many])
 
     arrive(3, 4)
     for k in range(nk):
@@ -318,9 +346,9 @@
                 own[j, f + m] = y[j * fp : (j + 1) * fp]
 
     arrive(8, 9)
-    picked = [roll(rim[...], elems // 2)] + [code[j : j + 1, :] for j in range(1, nj)]
+    lists = [roll(rim[...], elems // 2)] + [code[j : j + 1, :] for j in range(1, nj)]
     maps, hots = [], []
-    for row in picked:
+    for row in lists:
         group = jnp.zeros_like(row)
         for k in range(1, nk):
             group = group + jnp.where(row >= k * elems, 1, 0)
@@ -351,14 +379,20 @@
                     total = jnp.where(which == k, y[k * fp : (k + 1) * fp], total)
                 store(f + m, total)
 
+    e_lane = lax.broadcasted_iota(jnp.int32, (1, elems), 1)
+    lower = e_lane < elems // 2
+    fh = fp // 2
+
     def store_rim(f, total):
-        rim_send[f] = total
+        top, turned = total[:fh], roll(total[fh:], elems // 2)
+        rim_send[0, f] = jnp.where(lower, top, turned)
+        rim_send[1, f] = jnp.where(lower, turned, top)
 
     near_traces(0, store_rim)
 
-    @pl.when(early)
+    @pl.when(jnp.logical_not(corner))
     def _():
-        begin(rim_copies)
+        begin_rim()
 
     for j in range(1, nj):
 
@@ -368,14 +402,15 @@
         near_traces(j, store_near)
 
     for f in range(0, nf, many):
-        group = mixed(turn, f)
+        group = mixed(turn, range(f, f + many))
         for m in range(many):
             base[f + m] = group[m]
 
-    @pl.when(jnp.logical_not(early))
+    @pl.when(corner)
     def _():
-        pl.semaphore_wait(barrier, n_group + 1)
-        begin(par_copies + fric_copies + rim_copies)
+        pl.semaphore_wait(barrier, greeted)
+        begin(par_copies + fric_copies)
+        begin_rim()
 
     arrive(5, 6, 7)
     for j in range(nj):
@@ -417,10 +452,11 @@
 
     for copy in par_copies:
         copy.wait_recv()
-    slip = friction(normal_here, locked_here, par_recv[0], par_recv[1])
+    state = par_recv[:, 0].reshape(slots, 128)
+    slip = friction(normal_here, locked_here, state, par_recv[:, 1].reshape(slots, 128))
     signed = jnp.where(locked_here < 0.0, -slip, jnp.where(locked_here > 0.0, slip, 0.0))
-    for i in range(4):
-        slip_pad[i * slots : (i + 1) * slots, :nq] = signed
+    point = lax.broadcasted_iota(jnp.int32, (1, 128), 1)
+    signed = jnp.where(point < nq, signed, 0.0)
 
     arrive(12, 14, 15)
     for k in range(nface):
@@ -441,7 +477,7 @@
     locked = jnp.where(is_v1, mean, turned)
     drive_0 = jnp.where(is_v1, 0.5 * (roll(sides, 2 * slots) - sides), locked - sides)
     drive_1 = jnp.where(is_v1, 0.5 * sign_i, -1.0)
-    answer = slip_pad[...].T[:qp]
+    answer = jnp.concatenate([signed] * 4, axis=0).T[:qp]
     drive = drive_0 + drive_1 * answer
     high, low = halves(drive)
     gap = jnp.zeros((kq - qp, width), F32)
@@ -458,17 +494,14 @@
     )
     z = z[:cp] + z[cp:]
     by_traction, by_jump = z[:, :elems], z[:, elems:]
-    for copy in rim_copies:
-        copy.wait_recv()
-    e_lane = lax.broadcasted_iota(jnp.int32, (1, elems), 1)
-    has_prev = jnp.where(me_s > 0, 1, 0)
-    has_next = jnp.where(me_s < n_sub - 1, 1, 0)
-    from_prev = (e_lane < elems // 2) & (has_prev == 1)
-    from_next = (e_lane >= elems // 2) & (has_next == 1)
+    for copy, there in zip(rim_copies, (has_prev, has_next)):
+        pl.when(there)(copy.wait_recv)
+    from_prev = lower & has_prev
+    from_next = jnp.logical_not(lower) & has_next
     for f in range(nf):
-        near[0, f] = jnp.where(
-            from_prev, rim_recv[0, f], jnp.where(from_next, rim_recv[1, f], 0.0)
-        )
+        x, y = rim_recv[0, f], rim_recv[1, f]
+        for i, (x, y) in enumerate(((x, y), (roll(x, elems // 2), roll(y, elems // 2)))):
+            near[0, f, i * fh : (i + 1) * fh] = jnp.where(from_prev, x, jnp.where(from_next, y, 0.0))
     face_flux(0, 0, lambda g: near[0, g])
     high, low = halves(flux[:fp])
     l0 = lanes3(jnp.where(k_lane < fp, lift_all, 0.0), fp)[:, : 3 * fp]
@@ -484,11 +517,18 @@
     for copy in fric_copies:
         copy.wait_recv()
     state = par[0]
-    slip = friction(fric_recv[0], fric_recv[1], state, par[1])
+    slip = friction(
+        fric_recv[:, 0].reshape(slots, 128)[:, :nq],
+        fric_recv[:, 1].reshape(slots, 128)[:, :nq],
+        state,
+        par[1],
+    )
     out_state[...] = state + 0.5 * evolution_rate[...] * (jnp.exp(-state) - slip)
 
-    for copy in par_copies + fric_copies + rim_copies:
+    for copy in par_copies + fric_copies:
         copy.wait_send()
+    for copy, there in zip(rim_copies, (has_next, has_prev)):
+        pl.when(there)(copy.wait_send)
 
 
 def finish(dofs, state, out, out_state, sem):
@@ -546,12 +586,11 @@
             pltpu.VMEM((nface, cp, 128), F32),
             pltpu.VMEM((nface * cp, 128), F32),
             pltpu.VMEM((128, 128), F32),
-            pltpu.VMEM((nf, fp, elems), F32),
-            pltpu.VMEM((2, nf, fp, elems), F32),
-            pltpu.VMEM((2, slots, nq), F32),
-            pltpu.VMEM((2, slots, nq), F32),
-            pltpu.VMEM((2, slots, nq), F32),
-            pltpu.VMEM((width, 128), F32),
+            pltpu.VMEM((2, nf, fp // 2, elems), F32),
+            pltpu.VMEM((2, nf, fp // 2, elems), F32),
+        ]
+        + [pltpu.VMEM((n_group, 2, CAP, 128), F32)] * 4
+        + [
             pltpu.SemaphoreType.DMA((len(args),)),
             pltpu.SemaphoreType.DMA((copies,)),
             pltpu.SemaphoreType.DMA((copies,)),

time: 13.2 us -> 12 us (0.909)
  Pallas kernels: 12.4 us -> 11.2 us
    pallas_call x1, Pallas kernels: 11.7 us -> 10.5 us  [body(): pl.pallas_call(functools.partial(kernel, n_group, n_sub), out_shape=tuple...]
where the time goes in v3:
time: 12 us; the launch traced here: 11.9 us
  Pallas kernels  11.2 us (93%)
  between operations  0.65 us (5%)
    pallas_call x1, Pallas kernels, body(): pl.pallas_call(functools.partial(kernel, n_group, n_sub), out_shape=tuple...  10.5 us
    pallas_call x1, Pallas kernels, body(): pl.pallas_call(finish, out_shape=tuple((jax.ShapeDtypeStruct(s, F32) for...  0.69 us

profile of v3, /device:TPU:0, one launch (start us, length us, event | category | flops | bytes accessed | tf_op | source)
XLA Modules:
  0.0 11.9 jit_solution(5878960755373528294)
XLA Ops:
  0.6 10.5 %shard_map.194 = (f32[9,35,128]{2,1,0:T(8,128)S(1)}, f32[32,49]{1,0:T(8,128)S(1)}) custom-call(f32[9,35,128]{2,1,0:T(8,128)} %refs_0_.1, f32[9,9,3,128]{3,2,1,0:T(4,128)} %bitcast.14, f32[3,35,35]{2,1,0:T(8,128)} %refs_2_.1, f32[15,4,35]{2,1,0:T(4,128)} %bitcast.19, f32[12,15,35]{2,1,0:T(8,128)} %refs_4_.1, f32[9,9,4,128]{3,2,1,0:T(4,128)} %bitcast.15, ...), custom_call_target="tpu_custom_call" | custom-call | tf_op jit(solution)/shard_map/pallas_call | solution.py:567
  11.2 0.7 %shard_map.195 = (f32[9,35,128]{2,1,0:T(8,128)}, f32[32,49]{1,0:T(8,128)}) custom-call(f32[9,35,128]{2,1,0:T(8,128)S(1)} %get-tuple-element.6.dofs, f32[32,49]{1,0:T(8,128)S(1)} %get-tuple-element.7.state), custom_call_target="tpu_custom_call" | custom-call | tf_op jit(solution)/shard_map/pallas_call | solution.py:600

commit v4 on v3

--- a/solution.py
+++ b/solution.py
@@ -62,6 +62,9 @@
 
 N_IN = 19
 ORDER = (2, 0, 1, 13, 10, 11, 16, 17, 4, 3, 9, 8, 7, 14, 18, 12, 15, 5, 6)
+
+TOGETHER = ((2,), (0,), (1,), (10, 11, 13, 16, 17), (3, 4, 8, 9), (5, 6, 7), (12, 14, 15, 18))
+SEM = {i: n for n, members in enumerate(TOGETHER) for i in members}
 
 
 def kernel(n_group, n_sub, *refs):
@@ -110,7 +113,7 @@
     greeted = n_group - 1 + jnp.where(has_prev, 1, 0) + jnp.where(has_next, 1, 0)
 
     held = list(local[:16]) + [par.at[0], par.at[1]] + list(local[16:])
-    staged = {i: pltpu.make_async_copy(hbm[i], held[i], stage_sem.at[i]) for i in ORDER}
+    staged = {i: pltpu.make_async_copy(hbm[i], held[i], stage_sem.at[SEM[i]]) for i in ORDER}
     for i in ORDER:
         staged[i].start()
 
@@ -194,6 +197,8 @@
             pl.when(there)(copy.start)
 
     first_row = me_g == 0
+    far = me_g >= max(n_group // 2, 1)
+    middle = jnp.logical_not(first_row | far)
     corner = first_row & (me_s == 0)
 
     arrive(2)
@@ -232,7 +237,17 @@
             parts[0, f + m] = r[:, m * elems : (m + 1) * elems]
 
     arrive(1)
-    arrive(10, 11, 13)
+    arrive(10, 11, 13, 16, 17)
+    for o in range(n_group):
+        for i in range(2):
+            par_send[o, i, :, :nq] = par[i, o * CAP : (o + 1) * CAP, :]
+    par_recv[me_g] = par_send[me_g]
+
+    @pl.when(far)
+    def _():
+        pl.semaphore_wait(barrier, greeted)
+        begin(par_copies)
+
     for k in range(nface):
         for b in range(nb):
             w_ftrace[k, b : b + 1, :nq] = fault_trace[b, pl.ds(k, 1), :]
@@ -254,6 +269,14 @@
         a_fault.append(jnp.concatenate([high, low, high, gap], axis=0).T[:qp])
     a_fault = jnp.concatenate(a_fault, axis=0).astype(BF16)
 
+    half_hot = 0.5 * hot
+    weights = (
+        jnp.where(is_v1, 0.0, half_hot),
+        jnp.where(is_v1, half_hot, 0.0),
+        jnp.where(is_v1, sign_i * half_hot, 0.0),
+    )
+    mixing = jnp.concatenate([w for w in weights for _ in range(2)], axis=0).astype(BF16)
+    hot_16 = hot.astype(BF16)
     factorial = 1.0
     for degree in range(1, DERIV):
         factorial = factorial * (degree + 1)
@@ -266,13 +289,7 @@
             for m in range(many):
                 parts[1 - turn, f + m] = r[:, m * elems : (m + 1) * elems]
         if degree == 2:
-            arrive(16, 17)
-            for o in range(n_group):
-                for i in range(2):
-                    par_send[o, i, :, :nq] = par[i, o * CAP : (o + 1) * CAP, :]
-            par_recv[me_g] = par_send[me_g]
-
-            @pl.when(jnp.logical_not(first_row))
+            @pl.when(middle)
             def _():
                 pl.semaphore_wait(barrier, greeted)
                 begin(par_copies)
@@ -286,11 +303,6 @@
     picked = (0, 3, 7)
     finished(picked)
 
-    i0, i3, i7 = integ[0], integ[3], integ[7]
-    highs, lows = zip(*[halves(x) for x in (i0, i3, i7)])
-    g = mul(stacked(list(highs) + list(lows), 6 * cp), hot.astype(BF16))
-    g = g[: 3 * cp] + g[3 * cp :]
-    g0, g3, g7 = g[:cp], g[cp : 2 * cp], g[2 * cp :]
     def fault_sides(x):
         high, low = halves(x)
         y = mul(a_fault, stacked([high, high, low], 128))
@@ -299,7 +311,9 @@
             total = jnp.where(face_row == k, y[k * qp : (k + 1) * qp], total)
         return total
 
-    mean = fault_sides(jnp.where(is_v1, 0.5 * g3 + (0.5 * sign_i) * g7, 0.5 * g0))
+    tall = up(cp, 16)
+    split = [stacked([p], tall) for f in picked for p in halves(integ[f])]
+    mean = fault_sides(mul(jnp.concatenate(split, axis=1), mixing)[:cp])
     mean = mean + roll(mean, 2 * slots)
     mean_t = jnp.concatenate([mean, jnp.zeros((128 - qp, width), F32)], axis=0).T
     normal_here = mean_t[:slots]
@@ -318,12 +332,15 @@
         pl.semaphore_wait(barrier, greeted)
         begin(par_copies + fric_copies)
 
-    sides = fault_sides(jnp.where(is_v1, g7, g3))
+    highs, lows = zip(*[halves(integ[f]) for f in picked[1:]])
+    g = mul(stacked(list(highs) + list(lows), 4 * cp), hot_16)
+    g = g[: 2 * cp] + g[2 * cp :]
+    sides = fault_sides(jnp.where(is_v1, g[cp:], g[:cp]))
     rest = [f for f in range(nf) if f not in picked]
     for i in range(0, len(rest), many):
         finished(rest[i : i + many])
 
-    arrive(3, 4)
+    arrive(3, 4, 8, 9)
     for k in range(nk):
         w_near[k * fp : k * fp + nfm, :nb] = neighbour_trace[k]
     for j in range(nj):
@@ -345,7 +362,6 @@
             for j in range(nj):
                 own[j, f + m] = y[j * fp : (j + 1) * fp]
 
-    arrive(8, 9)
     lists = [roll(rim[...], elems // 2)] + [code[j : j + 1, :] for j in range(1, nj)]
     maps, hots = [], []
     for row in lists:
@@ -458,7 +474,7 @@
     point = lax.broadcasted_iota(jnp.int32, (1, 128), 1)
     signed = jnp.where(point < nq, signed, 0.0)
 
-    arrive(12, 14, 15)
+    arrive(12, 14, 15, 18)
     for k in range(nface):
         for b in range(nb):
             w_flift[k * cp + b : k * cp + b + 1, :nq] = fault_lift[b, pl.ds(k, 1), :]
@@ -513,7 +529,6 @@
         out[f] = dofs[f] + total[:nb]
 
 
-    arrive(18)
     for copy in fric_copies:
         copy.wait_recv()
     state = par[0]
@@ -591,7 +606,7 @@
         ]
         + [pltpu.VMEM((n_group, 2, CAP, 128), F32)] * 4
         + [
-            pltpu.SemaphoreType.DMA((len(args),)),
+            pltpu.SemaphoreType.DMA((len(TOGETHER),)),
             pltpu.SemaphoreType.DMA((copies,)),
             pltpu.SemaphoreType.DMA((copies,)),
         ],

time: 12 us -> 11.9 us (level)
    pallas_call x1, Pallas kernels: 10.5 us -> 10.4 us  [body(): pl.pallas_call(functools.partial(kernel, n_group, n_sub), out_shape=tuple...]
where the time goes in v4:
time: 11.9 us; the launch traced here: 11.7 us
  Pallas kernels  11.1 us (93%)
  between operations  0.65 us (5%)
    pallas_call x1, Pallas kernels, body(): pl.pallas_call(functools.partial(kernel, n_group, n_sub), out_shape=tuple...  10.4 us
    pallas_call x1, Pallas kernels, body(): pl.pallas_call(finish, out_shape=tuple((jax.ShapeDtypeStruct(s, F32) for...  0.69 us

profile of v4, /device:TPU:0, one launch (start us, length us, event | category | flops | bytes accessed | tf_op | source)
XLA Modules:
  0.0 11.7 jit_solution(12457635882035066075)
XLA Ops:
  0.6 10.4 %shard_map.194 = (f32[9,35,128]{2,1,0:T(8,128)S(1)}, f32[32,49]{1,0:T(8,128)S(1)}) custom-call(f32[9,35,128]{2,1,0:T(8,128)} %refs_0_.1, f32[9,9,3,128]{3,2,1,0:T(4,128)} %bitcast.14, f32[3,35,35]{2,1,0:T(8,128)} %refs_2_.1, f32[15,4,35]{2,1,0:T(4,128)} %bitcast.19, f32[12,15,35]{2,1,0:T(8,128)} %refs_4_.1, f32[9,9,4,128]{3,2,1,0:T(4,128)} %bitcast.15, ...), custom_call_target="tpu_custom_call" | custom-call | tf_op jit(solution)/shard_map/pallas_call | solution.py:582
  11.0 0.7 %shard_map.195 = (f32[9,35,128]{2,1,0:T(8,128)}, f32[32,49]{1,0:T(8,128)}) custom-call(f32[9,35,128]{2,1,0:T(8,128)S(1)} %get-tuple-element.6.dofs, f32[32,49]{1,0:T(8,128)S(1)} %get-tuple-element.7.state), custom_call_target="tpu_custom_call" | custom-call | tf_op jit(solution)/shard_map/pallas_call | solution.py:615

commit v5 on v4

--- a/solution.py
+++ b/solution.py
@@ -243,11 +243,6 @@
             par_send[o, i, :, :nq] = par[i, o * CAP : (o + 1) * CAP, :]
     par_recv[me_g] = par_send[me_g]
 
-    @pl.when(far)
-    def _():
-        pl.semaphore_wait(barrier, greeted)
-        begin(par_copies)
-
     for k in range(nface):
         for b in range(nb):
             w_ftrace[k, b : b + 1, :nq] = fault_trace[b, pl.ds(k, 1), :]
@@ -288,6 +283,13 @@
             r = mul(a_stiff, spread_out(group))
             for m in range(many):
                 parts[1 - turn, f + m] = r[:, m * elems : (m + 1) * elems]
+        if degree == 1:
+
+            @pl.when(far)
+            def _():
+                pl.semaphore_wait(barrier, greeted)
+                begin(par_copies)
+
         if degree == 2:
             @pl.when(middle)
             def _():
@@ -314,10 +316,10 @@
     tall = up(cp, 16)
     split = [stacked([p], tall) for f in picked for p in halves(integ[f])]
     mean = fault_sides(mul(jnp.concatenate(split, axis=1), mixing)[:cp])
-    mean = mean + roll(mean, 2 * slots)
     mean_t = jnp.concatenate([mean, jnp.zeros((128 - qp, width), F32)], axis=0).T
+    mean_t = mean_t[: 2 * slots] + mean_t[2 * slots :]
     normal_here = mean_t[:slots]
-    locked_here = mean_t[slots : 2 * slots]
+    locked_here = mean_t[slots:]
     for o in range(n_group):
         fric_send[o, 0] = normal_here[o * CAP : (o + 1) * CAP]
         fric_send[o, 1] = locked_here[o * CAP : (o + 1) * CAP]
@@ -332,10 +334,6 @@
         pl.semaphore_wait(barrier, greeted)
         begin(par_copies + fric_copies)
 
-    highs, lows = zip(*[halves(integ[f]) for f in picked[1:]])
-    g = mul(stacked(list(highs) + list(lows), 4 * cp), hot_16)
-    g = g[: 2 * cp] + g[2 * cp :]
-    sides = fault_sides(jnp.where(is_v1, g[cp:], g[:cp]))
     rest = [f for f in range(nf) if f not in picked]
     for i in range(0, len(rest), many):
         finished(rest[i : i + many])
@@ -343,25 +341,7 @@
     arrive(3, 4, 8, 9)
     for k in range(nk):
         w_near[k * fp : k * fp + nfm, :nb] = neighbour_trace[k]
-    for j in range(nj):
-        for q in range(nfm):
-            w_face[j * fp + q : j * fp + q + 1, :nb] = face_trace[q, pl.ds(j, 1), :]
-    gap = jnp.zeros((128 - cp, 128), F32)
-    v = [jnp.concatenate([w_stiff[d * cp : (d + 1) * cp], gap], axis=0).T[:cp] for d in range(ndim)]
-    a_last = jnp.concatenate(
-        [lanes3(jnp.concatenate(v, axis=0), cp), lanes3(w_face[...], cp)], axis=0
-    )
     a_near = lanes3(w_near[...], cp)
-    turn = DERIV % 2
-    for f in range(0, nf, many):
-        r = mul(a_last, spread_out([integ[f + m] for m in range(many)]))
-        for m in range(many):
-            y = r[:, m * elems : (m + 1) * elems]
-            parts[turn, f + m] = y[:rows]
-            y = y[rows:]
-            for j in range(nj):
-                own[j, f + m] = y[j * fp : (j + 1) * fp]
-
     lists = [roll(rim[...], elems // 2)] + [code[j : j + 1, :] for j in range(1, nj)]
     maps, hots = [], []
     for row in lists:
@@ -409,6 +389,28 @@
     @pl.when(jnp.logical_not(corner))
     def _():
         begin_rim()
+
+    highs, lows = zip(*[halves(integ[f]) for f in picked[1:]])
+    g = mul(stacked(list(highs) + list(lows), 4 * cp), hot_16)
+    g = g[: 2 * cp] + g[2 * cp :]
+    sides = fault_sides(jnp.where(is_v1, g[cp:], g[:cp]))
+    for j in range(nj):
+        for q in range(nfm):
+            w_face[j * fp + q : j * fp + q + 1, :nb] = face_trace[q, pl.ds(j, 1), :]
+    gap = jnp.zeros((128 - cp, 128), F32)
+    v = [jnp.concatenate([w_stiff[d * cp : (d + 1) * cp], gap], axis=0).T[:cp] for d in range(ndim)]
+    a_last = jnp.concatenate(
+        [lanes3(jnp.concatenate(v, axis=0), cp), lanes3(w_face[...], cp)], axis=0
+    )
+    turn = DERIV % 2
+    for f in range(0, nf, many):
+        r = mul(a_last, spread_out([integ[f + m] for m in range(many)]))
+        for m in range(many):
+            y = r[:, m * elems : (m + 1) * elems]
+            parts[turn, f + m] = y[:rows]
+            y = y[rows:]
+            for j in range(nj):
+                own[j, f + m] = y[j * fp : (j + 1) * fp]
 
     for j in range(1, nj):
 
@@ -489,6 +491,7 @@
     f_hi, f_lo = halves(w_flift[...])
     kq = 64
     a_lift = jnp.concatenate([f_hi + roll(f_lo, kq), f_hi], axis=1)[:, : 3 * kq].astype(BF16)
+    mean = mean + roll(mean, 2 * slots)
     turned = roll(mean, slots)
     locked = jnp.where(is_v1, mean, turned)
     drive_0 = jnp.where(is_v1, 0.5 * (roll(sides, 2 * slots) - sides), locked - sides)

time: 11.9 us -> 11.9 us (level)
  no operation moved by 1% of the time
where the time goes in v5:
time: 11.9 us; the launch traced here: 11.8 us
  Pallas kernels  11.1 us (93%)
  between operations  0.65 us (5%)
    pallas_call x1, Pallas kernels, body(): pl.pallas_call(functools.partial(kernel, n_group, n_sub), out_shape=tuple...  10.5 us
    pallas_call x1, Pallas kernels, body(): pl.pallas_call(finish, out_shape=tuple((jax.ShapeDtypeStruct(s, F32) for...  0.69 us

profile of v5, /device:TPU:0, one launch (start us, length us, event | category | flops | bytes accessed | tf_op | source)
XLA Modules:
  0.0 11.8 jit_solution(6511792262885079244)
XLA Ops:
  0.6 10.5 %shard_map.194 = (f32[9,35,128]{2,1,0:T(8,128)S(1)}, f32[32,49]{1,0:T(8,128)S(1)}) custom-call(f32[9,35,128]{2,1,0:T(8,128)} %refs_0_.1, f32[9,9,3,128]{3,2,1,0:T(4,128)} %bitcast.14, f32[3,35,35]{2,1,0:T(8,128)} %refs_2_.1, f32[15,4,35]{2,1,0:T(4,128)} %bitcast.19, f32[12,15,35]{2,1,0:T(8,128)} %refs_4_.1, f32[9,9,4,128]{3,2,1,0:T(4,128)} %bitcast.15, ...), custom_call_target="tpu_custom_call" | custom-call | tf_op jit(solution)/shard_map/pallas_call | solution.py:585
  11.1 0.7 %shard_map.195 = (f32[9,35,128]{2,1,0:T(8,128)}, f32[32,49]{1,0:T(8,128)}) custom-call(f32[9,35,128]{2,1,0:T(8,128)S(1)} %get-tuple-element.6.dofs, f32[32,49]{1,0:T(8,128)S(1)} %get-tuple-element.7.state), custom_call_target="tpu_custom_call" | custom-call | tf_op jit(solution)/shard_map/pallas_call | solution.py:618
